TPU v7x, 256 devices: a whole 4x4x8 slice. The times are simulated.
256 devices in a mesh: ctx: 32 (over z, y_lo, core), head: 8 (over x, y_hi).
Axes of the slice: x: 4, y: 4 (y_hi: 2, y_lo: 2; y = y_hi * 2 + y_lo), z: 8, core: 2. Of those that a mesh axis runs over, the one named last changes fastest.
Arguments:
- query: bfloat16 [4096, 8192], P('ctx', 'head'), may hold values from -11 to 11
- key_in: bfloat16 [4096, 1024], P('ctx', 'head'), may hold values from -11 to 11
- value: bfloat16 [4096, 1024], P('ctx', 'head'), may hold values from -6 to 6
- grad_y: bfloat16 [4096, 8192], P('ctx', 'head'), may hold values from -6 to 6
- w_out: bfloat16 [8192, 8192], P('head', 'ctx'), may hold values from -0.0625 to 0.0625
- parent: int32 [32], replicated, may hold values from 1 to 31, as said below
Outputs:
- grad_query: bfloat16 [4096, 8192], P('ctx', 'head')
- grad_key: bfloat16 [4096, 1024], P('ctx', 'head')
- grad_value: bfloat16 [4096, 1024], P('ctx', 'head')
Inputs may be any that keep to these rules, and one draw needn't show every extreme that they name: The shared prefix is blocks 32 - 4 to 31: parent[31] = 31 and parent[b] = b + 1 for the other prefix blocks; the earlier blocks form particles of 4 consecutive blocks, in which each block's parent is the block after it, except a particle's last block, whose parent is a block of the shared prefix.
All inputs are finite; a program needn't handle non-finite values.
Results may differ from a plain program's by a relative error of at most 0.014.
Values may be sent and summed in bfloat16 or wider, within the bound.
A program may use at most 128 MiB of HBM per device.

v0:
```python
import jax
import jax.numpy as jnp
from jax import lax
from jax.sharding import PartitionSpec as P

HPG = 8
DH = 128
BLOCK = 128


def shifted(value, axis, steps):
    count = lax.axis_size(axis)
    pairs = [(source, (source + steps) % count) for source in range(count)]
    return lax.ppermute(value, axis, pairs)


def ancestors(parent):
    count = parent.shape[0]
    index = jnp.arange(count, dtype=jnp.int32)
    start = (index[:, None] == index[None, :]).astype(jnp.int32)

    def advance(step, state):
        current, marks = state
        current = jnp.sum(jnp.where(current[:, None] == index[None, :], parent[None, :], 0), axis=1)
        marks = jnp.maximum(marks, (current[:, None] == index[None, :]).astype(jnp.int32))
        return (current, marks)

    return lax.fori_loop(0, count, advance, (index, start))[1]


def per_device(query, key_in, value, grad_y, w_out, parent):
    tokens_here = query.shape[0]
    groups = key_in.shape[1] // DH
    scale = DH ** (-0.5)
    cycle_size = lax.axis_size("ctx")
    place = lax.axis_index("ctx")
    full_rows = lax.all_gather(grad_y, "head", axis=1, tiled=True)
    grad_attn = lax.dot_general(
        full_rows,
        lax.all_gather(w_out, "ctx", axis=1, tiled=True),
        (((1,), (1,)), ((), ())),
        preferred_element_type=jnp.float32,
    ).astype(jnp.bfloat16)
    visible = ancestors(parent)
    block_count = parent.shape[0]
    blocks_here = tokens_here // BLOCK
    local_visible = lax.dynamic_slice_in_dim(visible, place * blocks_here, blocks_here, 0).astype(
        jnp.float32
    )
    query_pos = place * tokens_here + jnp.arange(tokens_here, dtype=jnp.int32)
    query_block = query_pos // BLOCK
    owned = place * blocks_here + jnp.arange(blocks_here, dtype=jnp.int32)
    query_select = (query_block[:, None] == owned[None, :]).astype(jnp.float32)
    query_visible = jnp.dot(query_select, local_visible)
    block_index = jnp.arange(block_count, dtype=jnp.int32)

    def make_mask(start, count):
        key_pos = start + jnp.arange(count, dtype=jnp.int32)
        key_block = key_pos // BLOCK
        key_select = (key_block[:, None] == block_index[None, :]).astype(jnp.float32)
        allowed = jnp.dot(query_visible, key_select.T) > 0.5
        return allowed & (
            (query_block[:, None] != key_block[None, :]) | (key_pos[None, :] <= query_pos[:, None])
        )

    query_heads = query.reshape(tokens_here, groups, HPG, DH).transpose(1, 2, 0, 3)
    grad_heads = grad_attn.reshape(tokens_here, groups, HPG, DH).transpose(1, 2, 0, 3)

    def split_heads(matrix):
        return matrix.reshape(matrix.shape[0], groups, DH).transpose(1, 0, 2)

    def join_heads(tensor):
        return tensor.transpose(1, 0, 2).reshape(tensor.shape[1], groups * DH)

    stat_shape = (groups, HPG, tokens_here)
    key_piece = lax.all_gather(key_in, "ctx", axis=0, tiled=True)
    value_piece = lax.all_gather(value, "ctx", axis=0, tiled=True)
    mask = make_mask(jnp.int32(0), key_piece.shape[0])
    statistics_top = jnp.full(stat_shape, -1e30, jnp.float32)
    scores = (
        jnp.einsum(
            "ghqd,gkd->ghqk",
            query_heads,
            split_heads(key_piece),
            preferred_element_type=jnp.float32,
        )
        * scale
    )
    masked = jnp.where(mask, scores, -1e30)
    new_top = jnp.maximum(statistics_top, jnp.max(masked, axis=3))
    weights = jnp.where(mask, jnp.exp(scores - new_top[..., None]), 0.0)
    dprob = jnp.einsum(
        "ghqd,gkd->ghqk", grad_heads, split_heads(value_piece), preferred_element_type=jnp.float32
    )
    statistics_norm = jnp.sum(weights, axis=3)
    weighted = jnp.sum(weights * dprob, axis=3)
    top, norm, weighted = (new_top, statistics_norm, weighted)
    delta = weighted / norm

    def contribution(key_piece, value_piece, mask):
        key_heads = split_heads(key_piece)
        value_heads = split_heads(value_piece)
        scores = (
            jnp.einsum("ghqd,gkd->ghqk", query_heads, key_heads, preferred_element_type=jnp.float32)
            * scale
        )
        prob = jnp.where(mask, jnp.exp(scores - top[..., None]), 0.0) / norm[..., None]
        dprob = jnp.einsum(
            "ghqd,gkd->ghqk", grad_heads, value_heads, preferred_element_type=jnp.float32
        )
        value_part = jnp.einsum(
            "ghqk,ghqd->gkd",
            prob.astype(jnp.bfloat16),
            grad_heads,
            preferred_element_type=jnp.float32,
        )
        dscore = (prob * (dprob - delta[..., None])).astype(jnp.bfloat16)
        query_part = (
            jnp.einsum("ghqk,gkd->ghqd", dscore, key_heads, preferred_element_type=jnp.float32)
            * scale
        )
        key_part = (
            jnp.einsum("ghqk,ghqd->gkd", dscore, query_heads, preferred_element_type=jnp.float32)
            * scale
        )
        return (query_part, join_heads(key_part), join_heads(value_part))

    def visit(key_piece, value_piece, start):
        mask = make_mask(start, key_piece.shape[0])
        return contribution(key_piece, value_piece, mask)

    grad_query = jnp.zeros((groups, HPG, tokens_here, DH), jnp.float32)

    def turn_one(step, state):
        grad_q, key_piece, value_piece, key_sum, value_sum = state
        owner = (place - step) % cycle_size
        query_part, key_part, value_part = visit(key_piece, value_piece, owner * tokens_here)
        grad_q = grad_q + query_part
        key_sum = key_sum + key_part
        value_sum = value_sum + value_part
        key_piece, value_piece = shifted((key_piece, value_piece), "ctx", 1)
        key_sum, value_sum = shifted((key_sum, value_sum), "ctx", 1)
        return (grad_q, key_piece, value_piece, key_sum, value_sum)

    zero_rows = jnp.zeros((tokens_here, groups * DH), jnp.float32)
    state = (grad_query, key_in, value, zero_rows, zero_rows)
    grad_query, unused_key, unused_value, grad_key, grad_value = lax.fori_loop(
        0, cycle_size, turn_one, state
    )
    grad_query = (
        grad_query.transpose(2, 0, 1, 3)
        .reshape(tokens_here, groups * HPG * DH)
        .astype(jnp.bfloat16)
    )
    return (grad_query, grad_key.astype(jnp.bfloat16), grad_value.astype(jnp.bfloat16))


def solution(mesh):
    placed = (
        P("ctx", "head"),
        P("ctx", "head"),
        P("ctx", "head"),
        P("ctx", "head"),
        P("head", "ctx"),
        P(),
    )
    return jax.shard_map(
        per_device,
        mesh=mesh,
        in_specs=placed,
        out_specs=(P("ctx", "head"), P("ctx", "head"), P("ctx", "head")),
        check_vma=False,
    )
```

profile of v0, /device:TPU:2, one launch (start us, length us, event | category | flops | bytes accessed | tf_op | source)
XLA Modules:
  0.0 608.8 jit_solution(9453911751109003068)
XLA Ops:
  12.1 29.5 %while.40 = (s32[]{:T(128)}, s32[32]{0:T(128)S(1)}, s32[32,32]{1,0:T(8,128)S(1)}, s32[32]{0:T(128)}, s32[]{:T(128)}) while((s32[]{:T(128)}, s32[32]{0:T(128)S(1)}, s32[32,32]{1,0:T(8,128)S(1)}, s32[32]{0:T(128)}, s32[]{:T(128)}) %tuple.80), condition=%wide.region_2.3_spmd.clone.clone, body=%wide.region_0.2_spmd.clone.clone.sunk | while | flops 6114 | bytes 9021 | solution.py:28
  43.7 33.4 %all-gather.5.cloned.1.call-done = bf16[4096,128]{1,0:T(8,128)(2,1)} async-done(((bf16[128,128]{1,0:T(8,128)(2,1)}), bf16[4096,128]{1,0:T(8,128)(2,1)}) %all-gather.5.cloned.1.call-update) | async-done | bytes 1048592 | tf_op jit(solution)/shard_map/all_gather | solution.py:76
  77.2 4.5 select_reduce_fusion.1
  81.7 5.7 copy-done
  87.4 4.9 fusion.35
  92.3 47.1 %all-gather.7.cloned.1.call-done = bf16[128,8192]{1,0:T(8,128)(2,1)} async-done(((bf16[128,1024]{1,0:T(8,128)(2,1)}), bf16[128,8192]{1,0:T(8,128)(2,1)}) %all-gather.7.cloned.1.call-update) | async-done | bytes 2097168 | tf_op jit(solution)/shard_map/all_gather | solution.py:37
  139.3 123.7 %all-gather.9.cloned.1.call-done = bf16[1024,8192]{1,0:T(8,128)(2,1)} async-done(((bf16[1024,256]{1,0:T(8,128)(2,1)}), bf16[1024,8192]{1,0:T(8,128)(2,1)}) %all-gather.9.cloned.1.call-update) | async-done | bytes 16777232 | tf_op jit(solution)/shard_map/all_gather | solution.py:40
  263.0 12.1 %fusion.38 = bf16[16,8,8,128]{3,1,2,0:T(8,128)(2,1)S(1)} fusion(bf16[128,8192]{1,0:T(8,128)(2,1)} %all-gather.7.cloned.1.call-done, bf16[1024,8192]{1,0:T(8,128)(2,1)} %all-gather.9.cloned.1.call-done), kind=kOutput, calls=%fused_computation.60 | convolution fusion | flops 2147614720 | bytes 19136512 | tf_op jit(solution)/shard_map/dot_general | solution.py:38
  275.2 52.8 %all-gather.11.cloned.1.call-done = bf16[4096,128]{1,0:T(8,128)(2,1)} async-done(((bf16[128,128]{1,0:T(8,128)(2,1)}), bf16[4096,128]{1,0:T(8,128)(2,1)}) %all-gather.11.cloned.1.call-update) | async-done | bytes 1048592 | tf_op jit(solution)/shard_map/all_gather | solution.py:77
  328.1 9.0 %multiply_reduce_fusion = f32[8,128]{1,0:T(8,128)S(1)} fusion(f32[8,128,4096]{2,1,0:T(8,128)} %copy-done, f32[8,128]{1,0:T(8,128)S(1)} %get-tuple-element.648, pred[128,4096]{1,0:T(8,128)(4,1)S(1)} %fusion.36, bf16[4096,128]{1,0:T(8,128)(2,1)} %all-gather.11.cloned.1.call-done, bf16[128,1,8,128]{3,2,0,1:T(8,128)(2,1)S(1)} %bitcast.121), kind=kOutput, calls=%fused_computation.51 | convolution fusion | flops 1094712320 | bytes 18620416 | tf_op jit(solution)/shard_map/ghqd,gkd->ghqk/dot_general | solution.py:92
  337.1 263.0 %while.41 = (s32[]{:T(128)}, f32[1,8,128,128]{3,2,1,0:T(8,128)S(1)}, bf16[128,128]{1,0:T(8,128)(2,1)S(1)}, bf16[128,128]{1,0:T(8,128)(2,1)S(1)}, f32[128,128]{1,...) while((s32[]{:T(128)}, ...), condition=%wide.region_7.8_spmd.clone.clone.clone, body=%wide.region_6.7_spmd.clone.clone.clone.sunk | while | flops 170405904 | bytes 5817452 | solution.py:147
  343.2 2.5 collective-permute-done.2
  373.7 2.6 collective-permute-done.1
  381.8 2.7 collective-permute-done.1
  397.4 2.5 collective-permute-start.3
  405.8 2.2 collective-permute-start.3
  422.2 2.2 collective-permute-start.3
  438.6 2.2 collective-permute-start.3
  454.9 2.2 collective-permute-start.3
  471.3 2.2 collective-permute-start.3
  487.6 2.2 collective-permute-start.3
  536.7 2.2 collective-permute-start.3
  553.0 2.2 collective-permute-start.3
  569.4 2.2 collective-permute-start.3
  (727 shorter events, 268.5 us)
Async XLA Ops:
  7.2 70.0 %all-gather.5.cloned.1.call-start = ((), (), s32[]{:S(2)}) async-start(), calls=%async_computation | async-start | bytes 1081344 | tf_op jit(solution)/shard_map/all_gather | solution.py:76
  10.0 129.4 %all-gather.7.cloned.1.call-start = ((), (), s32[]{:S(2)}) async-start(), calls=%async_computation.1 | async-start | bytes 2359296 | tf_op jit(solution)/shard_map/all_gather | solution.py:37
  10.7 252.3 %all-gather.9.cloned.1.call-start = ((), (), s32[]{:S(2)}) async-start(), calls=%async_computation.2 | async-start | bytes 17301504 | tf_op jit(solution)/shard_map/all_gather | solution.py:40
  11.5 316.6 %all-gather.11.cloned.1.call-start = ((), (), s32[]{:S(2)}) async-start(), calls=%async_computation.3 | async-start | bytes 1081344 | tf_op jit(solution)/shard_map/all_gather | solution.py:77
  348.3 6.2 %collective-permute-start.3 = (f32[128,128]{1,0:T(8,128)S(1)}, f32[128,128]{1,0:T(8,128)S(1)}, u32[]{:S(2)}, u32[]{:S(2)}) collective-permute-start(f32[128,128]{1,0:T(8,128)S(1)} %fusion.91), channel_id=1, source_target_pairs={{0,8},{8,16},{16,24},{24,32},{32,40},{40,48},{48,56},{56,64},{64,7... | collective-permute-start | bytes 196616 | tf_op jit(solution)/shard_map/while/body/eval_jaxpr/ppermute | solution.py:14
  356.5 6.2 %collective-permute-start.3 = (f32[128,128]{1,0:T(8,128)S(1)}, f32[128,128]{1,0:T(8,128)S(1)}, u32[]{:S(2)}, u32[]{:S(2)}) collective-permute-start(f32[128,128]{1,0:T(8,128)S(1)} %fusion.91), channel_id=1, source_target_pairs={{0,8},{8,16},{16,24},{24,32},{32,40},{40,48},{48,56},{56,64},{64,7... | collective-permute-start | bytes 196616 | tf_op jit(solution)/shard_map/while/body/eval_jaxpr/ppermute | solution.py:14
  364.7 6.2 %collective-permute-start.3 = (f32[128,128]{1,0:T(8,128)S(1)}, f32[128,128]{1,0:T(8,128)S(1)}, u32[]{:S(2)}, u32[]{:S(2)}) collective-permute-start(f32[128,128]{1,0:T(8,128)S(1)} %fusion.91), channel_id=1, source_target_pairs={{0,8},{8,16},{16,24},{24,32},{32,40},{40,48},{48,56},{56,64},{64,7... | collective-permute-start | bytes 196616 | tf_op jit(solution)/shard_map/while/body/eval_jaxpr/ppermute | solution.py:14
  372.9 6.2 %collective-permute-start.3 = (f32[128,128]{1,0:T(8,128)S(1)}, f32[128,128]{1,0:T(8,128)S(1)}, u32[]{:S(2)}, u32[]{:S(2)}) collective-permute-start(f32[128,128]{1,0:T(8,128)S(1)} %fusion.91), channel_id=1, source_target_pairs={{0,8},{8,16},{16,24},{24,32},{32,40},{40,48},{48,56},{56,64},{64,7... | collective-permute-start | bytes 196616 | tf_op jit(solution)/shard_map/while/body/eval_jaxpr/ppermute | solution.py:14
  381.0 6.2 %collective-permute-start.3 = (f32[128,128]{1,0:T(8,128)S(1)}, f32[128,128]{1,0:T(8,128)S(1)}, u32[]{:S(2)}, u32[]{:S(2)}) collective-permute-start(f32[128,128]{1,0:T(8,128)S(1)} %fusion.91), channel_id=1, source_target_pairs={{0,8},{8,16},{16,24},{24,32},{32,40},{40,48},{48,56},{56,64},{64,7... | collective-permute-start | bytes 196616 | tf_op jit(solution)/shard_map/while/body/eval_jaxpr/ppermute | solution.py:14
  389.2 6.2 %collective-permute-start.3 = (f32[128,128]{1,0:T(8,128)S(1)}, f32[128,128]{1,0:T(8,128)S(1)}, u32[]{:S(2)}, u32[]{:S(2)}) collective-permute-start(f32[128,128]{1,0:T(8,128)S(1)} %fusion.91), channel_id=1, source_target_pairs={{0,8},{8,16},{16,24},{24,32},{32,40},{40,48},{48,56},{56,64},{64,7... | collective-permute-start | bytes 196616 | tf_op jit(solution)/shard_map/while/body/eval_jaxpr/ppermute | solution.py:14
  397.4 6.2 %collective-permute-start.3 = (f32[128,128]{1,0:T(8,128)S(1)}, f32[128,128]{1,0:T(8,128)S(1)}, u32[]{:S(2)}, u32[]{:S(2)}) collective-permute-start(f32[128,128]{1,0:T(8,128)S(1)} %fusion.91), channel_id=1, source_target_pairs={{0,8},{8,16},{16,24},{24,32},{32,40},{40,48},{48,56},{56,64},{64,7... | collective-permute-start | bytes 196616 | tf_op jit(solution)/shard_map/while/body/eval_jaxpr/ppermute | solution.py:14
  405.8 6.1 %collective-permute-start.3 = (f32[128,128]{1,0:T(8,128)S(1)}, f32[128,128]{1,0:T(8,128)S(1)}, u32[]{:S(2)}, u32[]{:S(2)}) collective-permute-start(f32[128,128]{1,0:T(8,128)S(1)} %fusion.91), channel_id=1, source_target_pairs={{0,8},{8,16},{16,24},{24,32},{32,40},{40,48},{48,56},{56,64},{64,7... | collective-permute-start | bytes 196616 | tf_op jit(solution)/shard_map/while/body/eval_jaxpr/ppermute | solution.py:14
  414.0 6.1 %collective-permute-start.3 = (f32[128,128]{1,0:T(8,128)S(1)}, f32[128,128]{1,0:T(8,128)S(1)}, u32[]{:S(2)}, u32[]{:S(2)}) collective-permute-start(f32[128,128]{1,0:T(8,128)S(1)} %fusion.91), channel_id=1, source_target_pairs={{0,8},{8,16},{16,24},{24,32},{32,40},{40,48},{48,56},{56,64},{64,7... | collective-permute-start | bytes 196616 | tf_op jit(solution)/shard_map/while/body/eval_jaxpr/ppermute | solution.py:14
  422.2 6.1 %collective-permute-start.3 = (f32[128,128]{1,0:T(8,128)S(1)}, f32[128,128]{1,0:T(8,128)S(1)}, u32[]{:S(2)}, u32[]{:S(2)}) collective-permute-start(f32[128,128]{1,0:T(8,128)S(1)} %fusion.91), channel_id=1, source_target_pairs={{0,8},{8,16},{16,24},{24,32},{32,40},{40,48},{48,56},{56,64},{64,7... | collective-permute-start | bytes 196616 | tf_op jit(solution)/shard_map/while/body/eval_jaxpr/ppermute | solution.py:14
  438.6 6.1 %collective-permute-start.3 = (f32[128,128]{1,0:T(8,128)S(1)}, f32[128,128]{1,0:T(8,128)S(1)}, u32[]{:S(2)}, u32[]{:S(2)}) collective-permute-start(f32[128,128]{1,0:T(8,128)S(1)} %fusion.91), channel_id=1, source_target_pairs={{0,8},{8,16},{16,24},{24,32},{32,40},{40,48},{48,56},{56,64},{64,7... | collective-permute-start | bytes 196616 | tf_op jit(solution)/shard_map/while/body/eval_jaxpr/ppermute | solution.py:14
  454.9 6.1 %collective-permute-start.3 = (f32[128,128]{1,0:T(8,128)S(1)}, f32[128,128]{1,0:T(8,128)S(1)}, u32[]{:S(2)}, u32[]{:S(2)}) collective-permute-start(f32[128,128]{1,0:T(8,128)S(1)} %fusion.91), channel_id=1, source_target_pairs={{0,8},{8,16},{16,24},{24,32},{32,40},{40,48},{48,56},{56,64},{64,7... | collective-permute-start | bytes 196616 | tf_op jit(solution)/shard_map/while/body/eval_jaxpr/ppermute | solution.py:14
  471.3 6.1 %collective-permute-start.3 = (f32[128,128]{1,0:T(8,128)S(1)}, f32[128,128]{1,0:T(8,128)S(1)}, u32[]{:S(2)}, u32[]{:S(2)}) collective-permute-start(f32[128,128]{1,0:T(8,128)S(1)} %fusion.91), channel_id=1, source_target_pairs={{0,8},{8,16},{16,24},{24,32},{32,40},{40,48},{48,56},{56,64},{64,7... | collective-permute-start | bytes 196616 | tf_op jit(solution)/shard_map/while/body/eval_jaxpr/ppermute | solution.py:14
  487.6 6.1 %collective-permute-start.3 = (f32[128,128]{1,0:T(8,128)S(1)}, f32[128,128]{1,0:T(8,128)S(1)}, u32[]{:S(2)}, u32[]{:S(2)}) collective-permute-start(f32[128,128]{1,0:T(8,128)S(1)} %fusion.91), channel_id=1, source_target_pairs={{0,8},{8,16},{16,24},{24,32},{32,40},{40,48},{48,56},{56,64},{64,7... | collective-permute-start | bytes 196616 | tf_op jit(solution)/shard_map/while/body/eval_jaxpr/ppermute | solution.py:14
  504.0 6.1 %collective-permute-start.3 = (f32[128,128]{1,0:T(8,128)S(1)}, f32[128,128]{1,0:T(8,128)S(1)}, u32[]{:S(2)}, u32[]{:S(2)}) collective-permute-start(f32[128,128]{1,0:T(8,128)S(1)} %fusion.91), channel_id=1, source_target_pairs={{0,8},{8,16},{16,24},{24,32},{32,40},{40,48},{48,56},{56,64},{64,7... | collective-permute-start | bytes 196616 | tf_op jit(solution)/shard_map/while/body/eval_jaxpr/ppermute | solution.py:14
  520.3 6.1 %collective-permute-start.3 = (f32[128,128]{1,0:T(8,128)S(1)}, f32[128,128]{1,0:T(8,128)S(1)}, u32[]{:S(2)}, u32[]{:S(2)}) collective-permute-start(f32[128,128]{1,0:T(8,128)S(1)} %fusion.91), channel_id=1, source_target_pairs={{0,8},{8,16},{16,24},{24,32},{32,40},{40,48},{48,56},{56,64},{64,7... | collective-permute-start | bytes 196616 | tf_op jit(solution)/shard_map/while/body/eval_jaxpr/ppermute | solution.py:14
  536.7 6.1 %collective-permute-start.3 = (f32[128,128]{1,0:T(8,128)S(1)}, f32[128,128]{1,0:T(8,128)S(1)}, u32[]{:S(2)}, u32[]{:S(2)}) collective-permute-start(f32[128,128]{1,0:T(8,128)S(1)} %fusion.91), channel_id=1, source_target_pairs={{0,8},{8,16},{16,24},{24,32},{32,40},{40,48},{48,56},{56,64},{64,7... | collective-permute-start | bytes 196616 | tf_op jit(solution)/shard_map/while/body/eval_jaxpr/ppermute | solution.py:14
  553.0 6.1 %collective-permute-start.3 = (f32[128,128]{1,0:T(8,128)S(1)}, f32[128,128]{1,0:T(8,128)S(1)}, u32[]{:S(2)}, u32[]{:S(2)}) collective-permute-start(f32[128,128]{1,0:T(8,128)S(1)} %fusion.91), channel_id=1, source_target_pairs={{0,8},{8,16},{16,24},{24,32},{32,40},{40,48},{48,56},{56,64},{64,7... | collective-permute-start | bytes 196616 | tf_op jit(solution)/shard_map/while/body/eval_jaxpr/ppermute | solution.py:14
  569.4 6.1 %collective-permute-start.3 = (f32[128,128]{1,0:T(8,128)S(1)}, f32[128,128]{1,0:T(8,128)S(1)}, u32[]{:S(2)}, u32[]{:S(2)}) collective-permute-start(f32[128,128]{1,0:T(8,128)S(1)} %fusion.91), channel_id=1, source_target_pairs={{0,8},{8,16},{16,24},{24,32},{32,40},{40,48},{48,56},{56,64},{64,7... | collective-permute-start | bytes 196616 | tf_op jit(solution)/shard_map/while/body/eval_jaxpr/ppermute | solution.py:14
  585.7 6.1 %collective-permute-start.3 = (f32[128,128]{1,0:T(8,128)S(1)}, f32[128,128]{1,0:T(8,128)S(1)}, u32[]{:S(2)}, u32[]{:S(2)}) collective-permute-start(f32[128,128]{1,0:T(8,128)S(1)} %fusion.91), channel_id=1, source_target_pairs={{0,8},{8,16},{16,24},{24,32},{32,40},{40,48},{48,56},{56,64},{64,7... | collective-permute-start | bytes 196616 | tf_op jit(solution)/shard_map/while/body/eval_jaxpr/ppermute | solution.py:14
  (111 other events, 750.8 us)
Sparse Core Ops, SparseCore 0:
  10.4 66.7 all-gather.4
  79.8 59.4 all-gather.6
  141.1 121.8 all-gather.8
  265.3 62.7 all-gather.10
where the time goes:
time: 610 us; the launch traced here: 609 us
  waiting for transfers between devices  383 us (63%)
  matrix products  84.8 us (14%)
  starting transfers between devices  73.6 us (12%)
  other arithmetic  36.2 us (6%)
  local copies, waits for them, and re-layouts  14.8 us (2%)
  between operations  14 us (2%)
    all_gather x1, waiting for transfers between devices, per_device(): lax.all_gather(w_out, 'ctx', axis=1, tiled=True)  124 us
    ppermute x128, waiting for transfers between devices, shifted(): return lax.ppermute(value, axis, pairs)  124 us
    ppermute x128, starting transfers between devices, shifted(): return lax.ppermute(value, axis, pairs)  73.5 us
    all_gather x1, waiting for transfers between devices, per_device(): value_piece = lax.all_gather(value, 'ctx', axis=0, tiled=True)  52.8 us
    all_gather x1, waiting for transfers between devices, per_device(): full_rows = lax.all_gather(grad_y, 'head', axis=1, tiled=True)  47.1 us
    all_gather x1, waiting for transfers between devices, per_device(): key_piece = lax.all_gather(key_in, 'ctx', axis=0, tiled=True)  33.4 us
    reduce_sum x32, other arithmetic, advance(): jnp.sum(jnp.where(current[:, None] == index[None, :], parent[None, :], 0)...  26.9 us
    dot_general x32, matrix products, contribution(): jnp.einsum('ghqd,gkd->ghqk', query_heads, key_heads, preferred_element_ty...  17.2 us
  transfers between devices with their start and end apart: 132, of which 132 were waited for; matrix products, arithmetic and copies ran while one was open for 19% of the time, Pallas kernels for 0%

commit v1 on v0

v1 whole, which is shorter than its diff:
```python
import functools

import jax
import jax.numpy as jnp
from jax import lax
from jax.experimental import pallas as pl
from jax.experimental.pallas import tpu as pltpu
from jax.sharding import PartitionSpec as P

DH = 128
HPG = 8
GROUP = 4
NZ = 8
NH = 8
ROWS = 16
BF16 = jnp.bfloat16
F32 = jnp.float32
MESH = pl.DeviceIdType.MESH


def dot_nt(a, b):
    return lax.dot_general(a, b, (((1,), (1,)), ((), ())), preferred_element_type=F32)


def dot_nn(a, b):
    return lax.dot_general(a, b, (((1,), (0,)), ((), ())), preferred_element_type=F32)


def kernel(
    q_hbm, k_hbm, v_hbm, g_hbm, w_hbm, parent_ref,
    dq_ref, dk_ref, dv_ref,
    q_v, kv, s1, a, bw, cb, sp, rp, ga, gat, qt, bias, pf, plow, ds, dt, dsend, r1, psend, r2, fin,
    loc, p1s, p1r, p2s, p2r, ags, agr, bs, br, kvs, kvr, pxs, pxr, rss, rsr, d1s, d1r, d2s, d2r,
):
    ctx = lax.axis_index("ctx")
    head = lax.axis_index("head")
    z = ctx // GROUP
    m = ctx % GROUP
    x = head // 2
    yh = head % 2
    scale = DH ** (-0.5)
    sends = []

    def at_head(h):
        return (ctx, h)

    def at_z(zz):
        return (zz * GROUP + m, head)

    def at_m(mm):
        return (z * GROUP + mm, head)

    def remote(src, dst, send_sem, recv_sem, device):
        return pltpu.make_async_remote_copy(
            src_ref=src, dst_ref=dst, send_sem=send_sem, recv_sem=recv_sem,
            device_id=device, device_id_type=MESH,
        )

    def send(src, dst, send_sem, recv_sem, device):
        copy = remote(src, dst, send_sem, recv_sem, device)
        copy.start()
        sends.append(copy)

    def arrived(dst, recv_sem, device):
        remote(dst, dst, loc.at[0], recv_sem, device).wait_recv()

    local = [
        pltpu.make_async_copy(k_hbm, kv.at[0, 2 * m], loc.at[0]),
        pltpu.make_async_copy(v_hbm, kv.at[1, 2 * m], loc.at[1]),
        pltpu.make_async_copy(g_hbm.at[pl.ds(head * ROWS, ROWS)], s1.at[head], loc.at[2]),
        pltpu.make_async_copy(q_hbm, q_v, loc.at[3]),
        pltpu.make_async_copy(w_hbm, bw.at[m], loc.at[4]),
    ]
    for copy in local:
        copy.start()

    barrier = pltpu.get_barrier_semaphore()
    for i in range(1, NH):
        pl.semaphore_signal(barrier, inc=1, device_id=at_head((head + i) % NH), device_id_type=MESH)
    for i in range(1, NZ):
        pl.semaphore_signal(barrier, inc=1, device_id=at_z((z + i) % NZ), device_id_type=MESH)
    for i in range(1, GROUP):
        pl.semaphore_signal(barrier, inc=1, device_id=at_m((m + i) % GROUP), device_id_type=MESH)
    pl.semaphore_wait(barrier, NH + NZ + GROUP - 3)

    core_mate = at_m(m + 1 - 2 * (m % 2))
    m_core = m + 1 - 2 * (m % 2)
    m_side = (m + 2) % GROUP
    m_far = (m_core + 2) % GROUP

    for i in range(1, NH):
        h = (head + i) % NH
        send(g_hbm.at[pl.ds(h * ROWS, ROWS)], s1.at[head], p1s.at[i], p1r.at[head], at_head(h))

    @pl.when(z == NZ - 1)
    def _():
        for i in range(NZ - 1):
            remote(k_hbm, kv.at[0, 2 * m + 1], pxs.at[0, i], pxr.at[0], at_z(i)).start()
            remote(v_hbm, kv.at[1, 2 * m + 1], pxs.at[1, i], pxr.at[1], at_z(i)).start()

    local[0].wait()
    local[1].wait()
    for i in range(1, GROUP):
        mm = (m + i) % GROUP
        for c in range(2):
            send(kv.at[c, 2 * m], kv.at[c, 2 * m], kvs.at[c, 0, i], kvr.at[c, 2 * m], at_m(mm))
    half = w_hbm.shape[0] // 2
    for r in range(2):
        part = pl.ds(r * half, half)
        if r == 0:
            send(w_hbm.at[part], bw.at[m, part], bs.at[0, r], br.at[m, r], at_m(m_side))
        send(w_hbm.at[part], bw.at[m, part], bs.at[1, r], br.at[m, r], core_mate)

    for i in range(NH):
        k = (head + i) % NH
        if i == 0:
            local[2].wait()
        else:
            arrived(s1.at[k], p1r.at[k], at_head(k))

        @pl.when(k == z)
        def _():
            pltpu.make_async_copy(s1.at[k], a.at[head, z], loc.at[5]).start()

        @pl.when(k != z)
        def _():
            remote(s1.at[k], a.at[head, z], p2s.at[k], p2r.at[z], at_z(k)).start()

    @pl.when(z == NZ - 1)
    def _():
        for c in range(2):
            pltpu.make_async_copy(kv.at[c, 2 * m], kv.at[c, 2 * m + 1], loc.at[6 + c]).start()
        for c in range(2):
            pltpu.make_async_copy(kv.at[c, 2 * m], kv.at[c, 2 * m + 1], loc.at[6 + c]).wait()

    @pl.when(z != NZ - 1)
    def _():
        for c in range(2):
            arrived(kv.at[c, 2 * m + 1], pxr.at[c], at_z(0))

    for i in range(1, GROUP):
        mm = (m + i) % GROUP
        for c in range(2):
            send(kv.at[c, 2 * m + 1], kv.at[c, 2 * m + 1], kvs.at[c, 1, i], kvr.at[c, 2 * m + 1], at_m(mm))
    part = pl.ds(half, half)
    send(w_hbm.at[part], bw.at[m, part], bs.at[0, 1], br.at[m, 1], at_m(m_side))

    shape = bias.shape
    row = lax.broadcasted_iota(jnp.int32, shape, 0)
    col = lax.broadcasted_iota(jnp.int32, shape, 1)
    key_block = col // (2 * DH)
    in_prefix = (col // DH) % 2
    within = col % DH
    own_kind = jnp.where(z == NZ - 1, 1, 0)
    root = jnp.where(z == NZ - 1, GROUP, parent_ref[z * GROUP + GROUP - 1] - (NZ - 1) * GROUP)
    own_part = (in_prefix == own_kind) & (
        (key_block > m) | ((key_block == m) & (within <= row))
    )
    allowed = own_part | ((in_prefix == 1) & (key_block >= root))
    bias[...] = jnp.where(allowed, 0.0, -1e30)
    local[3].wait()
    for h in range(HPG):
        cols = pl.ds(h * DH, DH)
        qt[:, cols] = q_v[:, cols].astype(F32).T.astype(BF16)

    for i in range(1, NZ):
        zz = (z + i) % NZ
        arrived(a.at[head, zz], p2r.at[zz], at_z(zz))
    pltpu.make_async_copy(s1.at[0], a.at[head, z], loc.at[5]).wait()

    def x_at(dx):
        return 2 * ((x + dx) % 4) + yh

    h_y = 2 * x + 1 - yh
    send(a.at[head], a.at[head], ags.at[0], agr.at[head], at_head(x_at(1)))
    send(a.at[head], a.at[head], ags.at[1], agr.at[head], at_head(x_at(3)))
    send(a.at[head], a.at[head], ags.at[2], agr.at[head], at_head(h_y))
    send(a.at[head], a.at[head], ags.at[3], agr.at[head], at_head(x_at(2)))

    for c in range(2):
        for i in range(1, GROUP):
            mm = (m + i) % GROUP
            for t in range(2):
                arrived(kv.at[c, 2 * mm + t], kvr.at[c, 2 * mm + t], at_m(mm))

    def forward_head(h, carry):
        cols = pl.ds(pl.multiple_of(h * DH, DH), DH)
        keys = kv[0].reshape(2 * GROUP * DH, DH)
        s = dot_nt(q_v[:, cols], keys) * scale + bias[...]
        w = jnp.exp(s - jnp.max(s, axis=1, keepdims=True))
        p = w * (1.0 / jnp.sum(w, axis=1, keepdims=True))
        pf[cols, :] = p
        plow[cols, :] = p.astype(BF16)
        return carry

    lax.fori_loop(0, HPG // 2, forward_head, 0)

    for r in range(2):
        part = pl.ds(r * half, half)
        arrived(bw.at[m_side, part], br.at[m_side, r], core_mate)
        send(bw.at[m_side, part], bw.at[m_side, part], bs.at[2, r], br.at[m_side, r], core_mate)

    lax.fori_loop(HPG // 2, HPG, forward_head, 0)

    local[4].wait()
    for r in range(2):
        part = pl.ds(r * half, half)
        arrived(bw.at[m_core, part], br.at[m_core, r], core_mate)
        arrived(bw.at[m_far, part], br.at[m_far, r], core_mate)

    up = at_z((z + 1) % NZ)
    down = at_z((z + NZ - 1) % NZ)
    width = s1.shape[2]
    steps = NZ // 2
    side = (pl.ds(0, width // 2), pl.ds(width // 2, width // 2))

    def head_of(j):
        dx = 0
        dy = 0
        for at, (vx, vy) in enumerate([(0, 0), (1, 0), (3, 0), (0, 1), (2, 0), (1, 1), (3, 1), (2, 1)]):
            hit = jnp.where(j == at, 1, 0)
            dx = dx + vx * hit
            dy = dy + vy * hit
        return 2 * ((x + dx) % 4) + (yh + dy) % 2

    def hop(j, d, s):
        where = (slice(None), side[d]) if s == 0 else (slice(None), slice(None))
        return remote(
            sp.at[(j, d, s) + where], rp.at[(j, d, s) + where], rss.at[j, d, s], rsr.at[j, d, s],
            up if d == 0 else down,
        )

    def slot(t, carry):
        for s in range(steps, 0, -1):
            j = t - s

            @pl.when((j >= 0) & (j < NH))
            def _():
                for d in range(2):
                    hop(j, d, s - 1).wait_recv()
                    if s < steps:
                        dest = (z + steps - s) % NZ if d == 0 else (z + steps + s) % NZ
                        mine = pl.ds(pl.multiple_of(dest * ROWS, ROWS), ROWS)
                        if s == 1:
                            other = side[1 - d]
                            sp[j, d, s, :, side[d]] = (
                                cb[j, mine, side[d]] + rp[j, d, 0, :, side[d]].astype(F32)
                            ).astype(BF16)
                            sp[j, d, s, :, other] = cb[j, mine, other].astype(BF16)
                        else:
                            sp[j, d, s] = (cb[j, mine, :] + rp[j, d, s - 1].astype(F32)).astype(BF16)
                        hop(j, d, s).start()
                if s == steps:
                    mine = pl.ds(pl.multiple_of(z * ROWS, ROWS), ROWS)
                    total = cb[j, mine, :] + rp[j, 0, s - 1].astype(F32) + rp[j, 1, s - 1].astype(F32)
                    place = pl.multiple_of(head_of(j) * ROWS, ROWS)
                    ga[pl.ds(place, ROWS), :] = total.astype(BF16)

        @pl.when(t < NH)
        def _():
            h = head_of(t)

            @pl.when(t > 0)
            def _():
                arrived(a.at[h], agr.at[h], at_head(h_y))

            @pl.when(t == 3)
            def _():
                remote(a.at[h], a.at[h], ags.at[4], agr.at[h], at_head(x_at(1))).start()
                remote(a.at[h], a.at[h], ags.at[5], agr.at[h], at_head(x_at(3))).start()

            @pl.when(t == 4)
            def _():
                remote(a.at[h], a.at[h], ags.at[6], agr.at[h], at_head(h_y)).start()

            wide = bw.shape[2]
            for n in range(width // wide):
                cols = pl.ds(n * wide, wide)
                acc = None
                for b in range(GROUP):
                    rows = a[h, :, :, pl.ds(b * wide, wide)].reshape(NZ * ROWS, wide)
                    term = dot_nt(rows, bw[b, cols, :])
                    acc = term if acc is None else acc + term
                cb[t, :, cols] = acc
            far = pl.ds(pl.multiple_of(((z + steps) % NZ) * ROWS, ROWS), ROWS)
            for d in range(2):
                sp[t, d, 0, :, side[d]] = cb[t, far, side[d]].astype(BF16)
                hop(t, d, 0).start()

        return carry

    lax.fori_loop(0, NH + steps, slot, 0)

    mates = [(m + i) % GROUP for i in range(1, GROUP)]

    def spread(c, scaled):
        for b in range(2 * GROUP):
            dsend[c, b] = (dt[c, :, pl.ds(b * DH, DH)] * scaled).astype(BF16)
        for i, mm in enumerate(mates):
            pair = pl.ds(2 * mm, 2)
            send(dsend.at[c, pair], r1.at[c, m], d1s.at[c, i], d1r.at[c, m], at_m(mm))

    for h in range(HPG):
        cols = pl.ds(h * DH, DH)
        gat[:, cols] = ga[:, cols].astype(F32).T.astype(BF16)
    dt[0] = dot_nn(gat[...], plow[...])
    spread(0, 1.0)

    def backward_head(h, carry):
        cols = pl.ds(pl.multiple_of(h * DH, DH), DH)
        values = kv[1].reshape(2 * GROUP * DH, DH)
        dprob = dot_nt(ga[:, cols], values)
        p = pf[cols, :]
        delta = jnp.sum(p * dprob, axis=1, keepdims=True)
        ds[cols, :] = (p * (dprob - delta)).astype(BF16)
        return carry

    lax.fori_loop(0, HPG, backward_head, 0)
    dt[1] = dot_nn(qt[...], ds[...])
    spread(1, scale)

    def query_head(h, carry):
        cols = pl.ds(pl.multiple_of(h * DH, DH), DH)
        keys = kv[0].reshape(2 * GROUP * DH, DH)
        dq_ref[:, cols] = (dot_nn(ds[cols, :], keys) * scale).astype(BF16)
        return carry

    lax.fori_loop(0, HPG, query_head, 0)

    last = at_z(NZ - 1)
    for c in range(2):
        scaled = scale if c else 1.0
        for t in range(2):
            cols = pl.ds(pl.multiple_of((2 * m + t) * DH, DH), DH)
            fin[c, t] = dt[c, :, cols] * scaled
        for mm in mates:
            arrived(r1.at[c, mm], d1r.at[c, mm], at_m(mm))
            for t in range(2):
                fin[c, t] = fin[c, t] + r1[c, mm, t].astype(F32)

        @pl.when(z != NZ - 1)
        def _():
            psend[c] = fin[c, 1].astype(BF16)
            remote(psend.at[c], r2.at[c, z], d2s.at[c], d2r.at[c, z], last).start()

    for c in range(2):
        @pl.when(z == NZ - 1)
        def _():
            fin[c, 0] = fin[c, 0] + fin[c, 1]
            for zz in range(NZ - 1):
                arrived(r2.at[c, zz], d2r.at[c, zz], at_z(zz))
                fin[c, 0] = fin[c, 0] + r2[c, zz].astype(F32)

        out = dk_ref if c else dv_ref
        out[...] = fin[c, 0].T.astype(BF16)

    for copy in sends:
        copy.wait_send()
    for k in range(NH):
        @pl.when(k != z)
        def _():
            remote(s1.at[k], a.at[head, z], p2s.at[k], p2r.at[z], up).wait_send()

    for i in range(4, 7):
        remote(a.at[head], a.at[head], ags.at[i], agr.at[head], up).wait_send()

    @pl.when(z == NZ - 1)
    def _():
        for i in range(NZ - 1):
            remote(k_hbm, kv.at[0, 2 * m + 1], pxs.at[0, i], pxr.at[0], up).wait_send()
            remote(v_hbm, kv.at[1, 2 * m + 1], pxs.at[1, i], pxr.at[1], up).wait_send()

    @pl.when(z != NZ - 1)
    def _():
        for c in range(2):
            remote(psend.at[c], r2.at[c, z], d2s.at[c], d2r.at[c, z], up).wait_send()

    def drain(j, carry):
        for d in range(2):
            for s in range(steps):
                hop(j, d, s).wait_send()
        return carry

    lax.fori_loop(0, NH, drain, 0)


def per_device(query, key_in, value, grad_y, w_out, parent):
    tokens, width = query.shape
    keys = 2 * GROUP * DH
    dma = pltpu.SemaphoreType.DMA
    anywhere = pl.BlockSpec(memory_space=pl.ANY)
    vmem = pl.BlockSpec(memory_space=pltpu.VMEM)
    return pl.pallas_call(
        kernel,
        out_shape=(
            jax.ShapeDtypeStruct(query.shape, BF16),
            jax.ShapeDtypeStruct(key_in.shape, BF16),
            jax.ShapeDtypeStruct(value.shape, BF16),
        ),
        in_specs=[anywhere] * 5 + [pl.BlockSpec(memory_space=pltpu.SMEM)],
        out_specs=(vmem, vmem, vmem),
        scratch_shapes=[
            pltpu.VMEM((tokens, width), BF16),
            pltpu.VMEM((2, 2 * GROUP, DH, DH), BF16),
            pltpu.VMEM((NH, ROWS, width), BF16),
            pltpu.VMEM((NH, NZ, ROWS, width), BF16),
            pltpu.VMEM((GROUP,) + w_out.shape, BF16),
            pltpu.VMEM((NH, tokens, width), F32),
            pltpu.VMEM((NH, 2, NZ // 2, ROWS, width), BF16),
            pltpu.VMEM((NH, 2, NZ // 2, ROWS, width), BF16),
            pltpu.VMEM((tokens, width), BF16),
            pltpu.VMEM((tokens, width), BF16),
            pltpu.VMEM((tokens, width), BF16),
            pltpu.VMEM((tokens, keys), F32),
            pltpu.VMEM((width, keys), F32),
            pltpu.VMEM((width, keys), BF16),
            pltpu.VMEM((width, keys), BF16),
            pltpu.VMEM((2, DH, keys), F32),
            pltpu.VMEM((2, 2 * GROUP, DH, DH), BF16),
            pltpu.VMEM((2, GROUP, 2, DH, DH), BF16),
            pltpu.VMEM((2, DH, DH), BF16),
            pltpu.VMEM((2, NZ, DH, DH), BF16),
            pltpu.VMEM((2, 2, DH, DH), F32),
            dma((8,)),
            dma((NH,)), dma((NH,)),
            dma((NH,)), dma((NZ,)),
            dma((7,)), dma((NH,)),
            dma((3, 2)), dma((GROUP, 2)),
            dma((2, 2, GROUP)), dma((2, 2 * GROUP)),
            dma((2, NZ)), dma((2,)),
            dma((NH, 2, NZ // 2)), dma((NH, 2, NZ // 2)),
            dma((2, GROUP)), dma((2, GROUP)),
            dma((2,)), dma((2, NZ)),
        ],
        compiler_params=pltpu.CompilerParams(
            collective_id=0, has_side_effects=True, vmem_limit_bytes=60 * 1024 * 1024
        ),
        name="tree_attention_backward",
    )(query, key_in, value, grad_y, w_out, parent)


def solution(mesh):
    placed = (
        P("ctx", "head"),
        P("ctx", "head"),
        P("ctx", "head"),
        P("ctx", "head"),
        P("head", "ctx"),
        P(),
    )
    return jax.shard_map(
        per_device,
        mesh=mesh,
        in_specs=placed,
        out_specs=(P("ctx", "head"), P("ctx", "head"), P("ctx", "head")),
        check_vma=False,
    )
```

time: 610 us -> 95.3 us (0.16)
  waiting for transfers between devices: 383 us -> 0 us
  Pallas kernels: 0 us -> 90.9 us
  matrix products: 84.8 us -> 0 us
  starting transfers between devices: 73.6 us -> 0 us
  other arithmetic: 36.2 us -> 0 us
  between operations: 14 us -> 0.65 us
  local copies, waits for them, and re-layouts: 14.8 us -> 3.06 us
    all_gather x4 -> x0, waiting for transfers between devices: 257 us -> none  [the longest x1 124 us: per_device(): lax.all_gather(w_out, 'ctx', axis=1, tiled=True)]
    ppermute x128 -> x0, waiting for transfers between devices: 124 us -> none  [shifted(): return lax.ppermute(value, axis, pairs)]
    pallas_call x0 -> x1, Pallas kernels: none -> 90.9 us  [per_device(): pl.pallas_call(kernel, out_shape=(jax.ShapeDtypeStruct(query.shape, BF16)...]
    dot_general x196 -> x0, matrix products: 84.8 us -> none  [the longest x32 17.2 us: contribution(): jnp.einsum('ghqd,gkd->ghqk', query_heads, key_heads, preferred_element_ty...]
    ppermute x128 -> x0, starting transfers between devices: 73.5 us -> none  [shifted(): return lax.ppermute(value, axis, pairs)]
    reduce_sum x33 -> x0, other arithmetic: 31.8 us -> none  [the longest x32 26.9 us: advance(): jnp.sum(jnp.where(current[:, None] == index[None, :], parent[None, :], 0)...]
    unnamed x12 -> x7, local copies, waits for them, and re-layouts: 10.6 us -> 3.06 us
  transfers between devices with their start and end apart: 132 -> 0, of which waited for: 132 -> 0; matrix products, arithmetic and copies ran while one was open for 19% -> 0% of each run, Pallas kernels for 0% -> 0%
where the time goes in v1:
time: 95.3 us; the launch traced here: 94.6 us
  Pallas kernels  90.9 us (95%)
  local copies, waits for them, and re-layouts  3.06 us (3%)
    pallas_call x1, Pallas kernels, per_device(): pl.pallas_call(kernel, out_shape=(jax.ShapeDtypeStruct(query.shape, BF16)...  90.9 us
    unnamed x7, local copies, waits for them, and re-layouts  3.06 us

profile of v1, /device:TPU:2, one launch (start us, length us, event | category | flops | bytes accessed | tf_op | source)
XLA Modules:
  0.0 94.6 jit_solution(17220183556681307350)
XLA Ops:
  0.6 90.9 %tree_attention_backward.1 = (bf16[128,1024]{1,0:T(8,128)(2,1)}, bf16[128,128]{1,0:T(8,128)(2,1)}, bf16[128,128]{1,0:T(8,128)(2,1)}) custom-call(bf16[128,1024]{1,0:T(8,128)(2,1)} %q_hbm.1, bf16[128,128]{1,0:T(8,128)(2,1)} %k_hbm.1, bf16[128,128]{1,0:T(8,128)(2,1)} %v_hbm.1, bf16[128,1024]{1,0:T(8,128)(2,1)} %g_hbm.1, bf16[1024,256]{1,0:T(8,128)(2,1)} %w_hbm.1, ...), custom_call_target="tpu_custom_call" | custom-call | tf_op jit(solution)/shard_map/tree_attention_backward/pallas_call | solution.py:393
  91.5 0.0 copy-start.1
  91.5 1.7 %copy.12 = bf16[128,1024]{1,0:T(8,128)(2,1)} copy(bf16[128,1024]{1,0:T(8,128)(2,1)} %get-tuple-element.6) | data formatting | bytes 524288
  93.2 0.0 copy-done.1
  93.2 0.0 copy-start
  93.2 0.6 copy.13
  93.8 0.2 copy-done
  94.0 0.6 copy.14
Async XLA Ops:
  91.5 1.7 %copy-start.1 = (bf16[128,128]{1,0:T(8,128)(2,1)S(1)}, bf16[128,128]{1,0:T(8,128)(2,1)}, u32[]{:S(2)}) copy-start(bf16[128,128]{1,0:T(8,128)(2,1)} %get-tuple-element.7) | copy-start | bytes 98308
  93.2 0.8 copy-start

commit v2 on v1

--- a/solution.py
+++ b/solution.py
@@ -13,6 +13,7 @@
 NZ = 8
 NH = 8
 ROWS = 16
+SKEW = 2
 BF16 = jnp.bfloat16
 F32 = jnp.float32
 MESH = pl.DeviceIdType.MESH
@@ -92,23 +93,12 @@
         h = (head + i) % NH
         send(g_hbm.at[pl.ds(h * ROWS, ROWS)], s1.at[head], p1s.at[i], p1r.at[head], at_head(h))
 
-    @pl.when(z == NZ - 1)
-    def _():
-        for i in range(NZ - 1):
-            remote(k_hbm, kv.at[0, 2 * m + 1], pxs.at[0, i], pxr.at[0], at_z(i)).start()
-            remote(v_hbm, kv.at[1, 2 * m + 1], pxs.at[1, i], pxr.at[1], at_z(i)).start()
-
-    local[0].wait()
-    local[1].wait()
-    for i in range(1, GROUP):
-        mm = (m + i) % GROUP
-        for c in range(2):
-            send(kv.at[c, 2 * m], kv.at[c, 2 * m], kvs.at[c, 0, i], kvr.at[c, 2 * m], at_m(mm))
     half = w_hbm.shape[0] // 2
     for r in range(2):
         part = pl.ds(r * half, half)
-        if r == 0:
-            send(w_hbm.at[part], bw.at[m, part], bs.at[0, r], br.at[m, r], at_m(m_side))
+        send(w_hbm.at[part], bw.at[m, part], bs.at[0, r], br.at[m, r], at_m(m_side))
+    for r in range(2):
+        part = pl.ds(r * half, half)
         send(w_hbm.at[part], bw.at[m, part], bs.at[1, r], br.at[m, r], core_mate)
 
     for i in range(NH):
@@ -128,22 +118,16 @@
 
     @pl.when(z == NZ - 1)
     def _():
-        for c in range(2):
-            pltpu.make_async_copy(kv.at[c, 2 * m], kv.at[c, 2 * m + 1], loc.at[6 + c]).start()
-        for c in range(2):
-            pltpu.make_async_copy(kv.at[c, 2 * m], kv.at[c, 2 * m + 1], loc.at[6 + c]).wait()
-
-    @pl.when(z != NZ - 1)
-    def _():
-        for c in range(2):
-            arrived(kv.at[c, 2 * m + 1], pxr.at[c], at_z(0))
-
+        for i in range(NZ - 1):
+            remote(k_hbm, kv.at[0, 2 * m + 1], pxs.at[0, i], pxr.at[0], at_z(i)).start()
+            remote(v_hbm, kv.at[1, 2 * m + 1], pxs.at[1, i], pxr.at[1], at_z(i)).start()
+
+    local[0].wait()
+    local[1].wait()
     for i in range(1, GROUP):
         mm = (m + i) % GROUP
         for c in range(2):
-            send(kv.at[c, 2 * m + 1], kv.at[c, 2 * m + 1], kvs.at[c, 1, i], kvr.at[c, 2 * m + 1], at_m(mm))
-    part = pl.ds(half, half)
-    send(w_hbm.at[part], bw.at[m, part], bs.at[0, 1], br.at[m, 1], at_m(m_side))
+            send(kv.at[c, 2 * m], kv.at[c, 2 * m], kvs.at[c, 0, i], kvr.at[c, 2 * m], at_m(mm))
 
     shape = bias.shape
     row = lax.broadcasted_iota(jnp.int32, shape, 0)
@@ -177,12 +161,6 @@
     send(a.at[head], a.at[head], ags.at[2], agr.at[head], at_head(h_y))
     send(a.at[head], a.at[head], ags.at[3], agr.at[head], at_head(x_at(2)))
 
-    for c in range(2):
-        for i in range(1, GROUP):
-            mm = (m + i) % GROUP
-            for t in range(2):
-                arrived(kv.at[c, 2 * mm + t], kvr.at[c, 2 * mm + t], at_m(mm))
-
     def forward_head(h, carry):
         cols = pl.ds(pl.multiple_of(h * DH, DH), DH)
         keys = kv[0].reshape(2 * GROUP * DH, DH)
@@ -193,14 +171,27 @@
         plow[cols, :] = p.astype(BF16)
         return carry
 
-    lax.fori_loop(0, HPG // 2, forward_head, 0)
-
     for r in range(2):
         part = pl.ds(r * half, half)
         arrived(bw.at[m_side, part], br.at[m_side, r], core_mate)
         send(bw.at[m_side, part], bw.at[m_side, part], bs.at[2, r], br.at[m_side, r], core_mate)
 
-    lax.fori_loop(HPG // 2, HPG, forward_head, 0)
+    @pl.when(z == NZ - 1)
+    def _():
+        for c in range(2):
+            pltpu.make_async_copy(kv.at[c, 2 * m], kv.at[c, 2 * m + 1], loc.at[6 + c]).start()
+        for c in range(2):
+            pltpu.make_async_copy(kv.at[c, 2 * m], kv.at[c, 2 * m + 1], loc.at[6 + c]).wait()
+
+    @pl.when(z != NZ - 1)
+    def _():
+        for c in range(2):
+            arrived(kv.at[c, 2 * m + 1], pxr.at[c], at_z(0))
+
+    for i in range(1, GROUP):
+        mm = (m + i) % GROUP
+        for c in range(2):
+            send(kv.at[c, 2 * m + 1], kv.at[c, 2 * m + 1], kvs.at[c, 1, i], kvr.at[c, 2 * m + 1], at_m(mm))
 
     local[4].wait()
     for r in range(2):
@@ -232,7 +223,7 @@
 
     def slot(t, carry):
         for s in range(steps, 0, -1):
-            j = t - s
+            j = t - SKEW * s
 
             @pl.when((j >= 0) & (j < NH))
             def _():
@@ -287,18 +278,32 @@
                 sp[t, d, 0, :, side[d]] = cb[t, far, side[d]].astype(BF16)
                 hop(t, d, 0).start()
 
+        @pl.when(t == NH - 1)
+        def _():
+            for c in range(2):
+                for i in range(1, GROUP):
+                    mm = (m + i) % GROUP
+                    for e in range(2):
+                        arrived(kv.at[c, 2 * mm + e], kvr.at[c, 2 * mm + e], at_m(mm))
+
+        @pl.when((t >= NH - 1) & (t < NH - 1 + HPG))
+        def _():
+            forward_head(t - (NH - 1), carry)
+
         return carry
 
-    lax.fori_loop(0, NH + steps, slot, 0)
+    lax.fori_loop(0, NH + SKEW * steps, slot, 0)
 
     mates = [(m + i) % GROUP for i in range(1, GROUP)]
 
     def spread(c, scaled):
         for b in range(2 * GROUP):
             dsend[c, b] = (dt[c, :, pl.ds(b * DH, DH)] * scaled).astype(BF16)
+        share(c, 1)
+
+    def share(c, e):
         for i, mm in enumerate(mates):
-            pair = pl.ds(2 * mm, 2)
-            send(dsend.at[c, pair], r1.at[c, m], d1s.at[c, i], d1r.at[c, m], at_m(mm))
+            send(dsend.at[c, 2 * mm + e], r1.at[c, m, e], d1s.at[c, e, i], d1r.at[c, e, m], at_m(mm))
 
     for h in range(HPG):
         cols = pl.ds(h * DH, DH)
@@ -318,6 +323,8 @@
     lax.fori_loop(0, HPG, backward_head, 0)
     dt[1] = dot_nn(qt[...], ds[...])
     spread(1, scale)
+    share(0, 0)
+    share(1, 0)
 
     def query_head(h, carry):
         cols = pl.ds(pl.multiple_of(h * DH, DH), DH)
@@ -328,15 +335,17 @@
     lax.fori_loop(0, HPG, query_head, 0)
 
     last = at_z(NZ - 1)
+
+    def collect(c, e):
+        cols = pl.ds(pl.multiple_of((2 * m + e) * DH, DH), DH)
+        total = dt[c, :, cols] * (scale if c else 1.0)
+        for mm in mates:
+            arrived(r1.at[c, mm, e], d1r.at[c, e, mm], at_m(mm))
+            total = total + r1[c, mm, e].astype(F32)
+        fin[c, e] = total
+
     for c in range(2):
-        scaled = scale if c else 1.0
-        for t in range(2):
-            cols = pl.ds(pl.multiple_of((2 * m + t) * DH, DH), DH)
-            fin[c, t] = dt[c, :, cols] * scaled
-        for mm in mates:
-            arrived(r1.at[c, mm], d1r.at[c, mm], at_m(mm))
-            for t in range(2):
-                fin[c, t] = fin[c, t] + r1[c, mm, t].astype(F32)
+        collect(c, 1)
 
         @pl.when(z != NZ - 1)
         def _():
@@ -344,12 +353,17 @@
             remote(psend.at[c], r2.at[c, z], d2s.at[c], d2r.at[c, z], last).start()
 
     for c in range(2):
+        collect(c, 0)
+
+    for c in range(2):
         @pl.when(z == NZ - 1)
         def _():
-            fin[c, 0] = fin[c, 0] + fin[c, 1]
-            for zz in range(NZ - 1):
+            total = fin[c, 0] + fin[c, 1]
+            for i in range(1, NZ):
+                zz = NZ - 1 - i
                 arrived(r2.at[c, zz], d2r.at[c, zz], at_z(zz))
-                fin[c, 0] = fin[c, 0] + r2[c, zz].astype(F32)
+                total = total + r2[c, zz].astype(F32)
+            fin[c, 0] = total
 
         out = dk_ref if c else dv_ref
         out[...] = fin[c, 0].T.astype(BF16)
@@ -429,7 +443,7 @@
             dma((2, 2, GROUP)), dma((2, 2 * GROUP)),
             dma((2, NZ)), dma((2,)),
             dma((NH, 2, NZ // 2)), dma((NH, 2, NZ // 2)),
-            dma((2, GROUP)), dma((2, GROUP)),
+            dma((2, 2, GROUP)), dma((2, 2, GROUP)),
             dma((2,)), dma((2, NZ)),
         ],
         compiler_params=pltpu.CompilerParams(

time: 95.3 us -> 83.6 us (0.88)
  Pallas kernels: 90.9 us -> 78.4 us
    pallas_call x1, Pallas kernels: 90.9 us -> 78.4 us  [per_device(): pl.pallas_call(kernel, out_shape=(jax.ShapeDtypeStruct(query.shape, BF16)...]
where the time goes in v2:
time: 83.6 us; the launch traced here: 82.1 us
  Pallas kernels  78.4 us (94%)
  local copies, waits for them, and re-layouts  3.06 us (4%)
    pallas_call x1, Pallas kernels, per_device(): pl.pallas_call(kernel, out_shape=(jax.ShapeDtypeStruct(query.shape, BF16)...  78.4 us
    unnamed x7, local copies, waits for them, and re-layouts  3.06 us

profile of v2, /device:TPU:2, one launch (start us, length us, event | category | flops | bytes accessed | tf_op | source)
XLA Modules:
  0.0 82.1 jit_solution(9334038187178065886)
XLA Ops:
  0.6 78.4 %tree_attention_backward.1 = (bf16[128,1024]{1,0:T(8,128)(2,1)}, bf16[128,128]{1,0:T(8,128)(2,1)}, bf16[128,128]{1,0:T(8,128)(2,1)}) custom-call(bf16[128,1024]{1,0:T(8,128)(2,1)} %q_hbm.1, bf16[128,128]{1,0:T(8,128)(2,1)} %k_hbm.1, bf16[128,128]{1,0:T(8,128)(2,1)} %v_hbm.1, bf16[128,1024]{1,0:T(8,128)(2,1)} %g_hbm.1, bf16[1024,256]{1,0:T(8,128)(2,1)} %w_hbm.1, ...), custom_call_target="tpu_custom_call" | custom-call | tf_op jit(solution)/shard_map/tree_attention_backward/pallas_call | solution.py:407
  79.0 0.0 copy-start.1
  79.0 1.7 %copy.12 = bf16[128,1024]{1,0:T(8,128)(2,1)} copy(bf16[128,1024]{1,0:T(8,128)(2,1)} %get-tuple-element.6) | data formatting | bytes 524288
  80.7 0.0 copy-done.1
  80.7 0.0 copy-start
  80.7 0.6 copy.13
  81.3 0.2 copy-done
  81.5 0.6 copy.14
Async XLA Ops:
  79.0 1.7 %copy-start.1 = (bf16[128,128]{1,0:T(8,128)(2,1)S(1)}, bf16[128,128]{1,0:T(8,128)(2,1)}, u32[]{:S(2)}) copy-start(bf16[128,128]{1,0:T(8,128)(2,1)} %get-tuple-element.7) | copy-start | bytes 98308
  80.7 0.8 copy-start
